TPU v7x, 32 devices: a whole 2x2x4 slice. The times are simulated.
32 devices in a mesh: groups: 2 (over y), ctx: 4 (over z), tp: 2 (over x), sub: 2 (over core).
Axes of the slice: x: 2, y: 2, z: 4, core: 2. Of those that a mesh axis runs over, the one named last changes fastest.
Arguments:
- queries: bfloat16 [3072, 8192], P(('groups', 'ctx'), ('tp', 'sub')), parts along dimension 0, may hold values from -200 to 200
- keys: bfloat16 [3072, 1024], P(('groups', 'ctx'), ('tp', 'sub')), parts along dimension 0, may hold values from -6 to 6
- values: bfloat16 [3072, 1024], P(('groups', 'ctx'), ('tp', 'sub')), parts along dimension 0, may hold values from -6 to 6
- segment_ids: int32 [3072], P(('groups', 'ctx')), parts along dimension 0, may hold values from 0 to 8, as said below
Outputs:
- attended: bfloat16 [3072, 8192], P(('groups', 'ctx'), ('tp', 'sub')), parts along dimension 0
There are 2 independent parts, one for each index of `groups`. A program takes and returns all parts, laid end to end along the dimension named above; each array names one. Nothing has to cross between parts.
Inputs may be any that keep to these rules, and one draw needn't show every extreme that they name: segment_ids is 0 on the first 384 tokens; after them exactly 8 chains 1, 2, ..., 8 follow in order and fill the row, each a run of 96 to 192 tokens, one of them exactly 192.
All inputs are finite; a program needn't handle non-finite values.
Results may differ from a plain program's by a relative error of at most 0.0041.
Values may be sent and summed in bfloat16 or wider, within the bound.
No kernel may reach another device: no remote copies, remote signals or barrier semaphores. Data moves between devices by JAX's collectives and lax.ppermute only.
A program may use at most 64 MiB of HBM per device.

v0:
```python
import jax
import jax.numpy as jnp
from jax import lax
from jax.sharding import PartitionSpec as P

HEAD_DIM = 128
GROUP = 8


def attend_block(
    running,
    key_block,
    value_block,
    segment_block,
    first_row,
    query_heads,
    query_places,
    query_segment,
):
    number = key_block.shape[0]
    heads_here = key_block.shape[1] // HEAD_DIM
    key_places = first_row + jnp.arange(number, dtype=jnp.int32)
    same = (segment_block[None, :] == query_segment[:, None]) | (segment_block[None, :] == 0)
    visible = (key_places[None, :] <= query_places[:, None]) & same
    key_heads = key_block.reshape(number, heads_here, HEAD_DIM)
    value_heads = value_block.reshape(number, heads_here, HEAD_DIM)

    def compute(state):
        row_peak, row_total, weighted = state
        scores = jnp.einsum(
            "qhgd,khd->hgqk", query_heads, key_heads, preferred_element_type=jnp.float32
        ) * HEAD_DIM ** (-0.5)
        scores = jnp.where(visible[None, None], scores, -1e30)
        new_peak = jnp.maximum(row_peak, jnp.max(scores, axis=-1))
        factor = jnp.exp(row_peak - new_peak)
        weights = jnp.where(visible[None, None], jnp.exp(scores - new_peak[..., None]), 0.0)
        new_total = row_total * factor + jnp.sum(weights, axis=-1)
        added = jnp.einsum(
            "hgqk,khd->hgqd",
            weights.astype(jnp.bfloat16),
            value_heads,
            preferred_element_type=jnp.float32,
        )
        return (new_peak, new_total, weighted * factor[..., None] + added)

    return lax.cond(jnp.any(visible), compute, lambda state: state, running)


def per_device(queries, keys, values, segment_ids):
    row_count = queries.shape[0]
    heads_here = keys.shape[1] // HEAD_DIM
    my_index = lax.axis_index("ctx")
    query_places = my_index * row_count + jnp.arange(row_count, dtype=jnp.int32)
    query_heads = queries.reshape(row_count, heads_here, GROUP, HEAD_DIM)
    initial = (
        jnp.full((heads_here, GROUP, row_count), -1e30, jnp.float32),
        jnp.zeros((heads_here, GROUP, row_count), jnp.float32),
        jnp.zeros((heads_here, GROUP, row_count, HEAD_DIM), jnp.float32),
    )
    key_all = lax.all_gather(keys, "ctx", axis=0, tiled=True)
    value_all = lax.all_gather(values, "ctx", axis=0, tiled=True)
    segment_all = lax.all_gather(segment_ids, "ctx", axis=0, tiled=True)
    blocks = max(1, key_all.shape[0] // row_count)
    width_rows = key_all.shape[0] // blocks

    def turn(number, state):
        offset = number * width_rows
        key_part = lax.dynamic_slice_in_dim(key_all, offset, width_rows, 0)
        value_part = lax.dynamic_slice_in_dim(value_all, offset, width_rows, 0)
        segment_part = lax.dynamic_slice_in_dim(segment_all, offset, width_rows, 0)
        return attend_block(
            state,
            key_part,
            value_part,
            segment_part,
            offset,
            query_heads,
            query_places,
            segment_ids,
        )

    final = lax.fori_loop(0, blocks, turn, initial)
    row_peak, row_total, weighted = final
    mixed = weighted / row_total[..., None]
    mixed = jnp.transpose(mixed, (2, 0, 1, 3)).reshape(row_count, heads_here * GROUP * HEAD_DIM)
    return mixed.astype(jnp.bfloat16)


def solution(mesh):
    placed = (
        P(("groups", "ctx"), ("tp", "sub")),
        P(("groups", "ctx"), ("tp", "sub")),
        P(("groups", "ctx"), ("tp", "sub")),
        P(("groups", "ctx")),
    )
    return jax.shard_map(
        per_device,
        mesh=mesh,
        in_specs=placed,
        out_specs=P(("groups", "ctx"), ("tp", "sub")),
        check_vma=False,
    )
```

profile of v0, /device:TPU:22, one launch (start us, length us, event | category | flops | bytes accessed | tf_op | source)
XLA Modules:
  0.0 98.1 jit_solution(1589817121826386383)
XLA Ops:
  0.0 0.7 reshape.39
  0.7 10.3 %all-gather = s32[4,1,384]{2,1,0:T(1,128)S(1)} all-gather(s32[1,1,384]{2,1,0:T(1,128)S(1)} %reshape.39), channel_id=1, replica_groups=mesh['groups'=2,'ctx'=4,'tp'=2,'sub'=2] {'ctx'}, dimensions={0}, use_global_device_ids=true | all-gather | bytes 7680 | tf_op jit(solution)/shard_map/all_gather | solution.py:62
  11.0 1.1 %copy.18 = bf16[384,256]{0,1:T(8,128)(2,1)S(1)} copy(bf16[384,256]{1,0:T(8,128)(2,1)} %param.9) | data formatting | bytes 393216 | tf_op args[1]
  12.1 1.1 %copy.20 = bf16[384,256]{0,1:T(8,128)(2,1)S(1)} copy(bf16[384,256]{1,0:T(8,128)(2,1)} %param.10) | data formatting | bytes 393216 | tf_op args[2]
  13.2 18.8 %all_gather.11 = bf16[1536,256]{0,1:T(8,128)(2,1)} all-gather(bf16[384,256]{0,1:T(8,128)(2,1)S(1)} %copy.20), channel_id=1, replica_groups=mesh['groups'=2,'ctx'=4,'tp'=2,'sub'=2] {'ctx'}, dimensions={0}, use_global_device_ids=true | all-gather | bytes 983040 | tf_op jit(solution)/shard_map/all_gather | solution.py:61
  32.0 17.9 %all_gather.10 = bf16[1536,256]{0,1:T(8,128)(2,1)} all-gather(bf16[384,256]{0,1:T(8,128)(2,1)S(1)} %copy.18), channel_id=1, replica_groups=mesh['groups'=2,'ctx'=4,'tp'=2,'sub'=2] {'ctx'}, dimensions={0}, use_global_device_ids=true | all-gather | bytes 983040 | tf_op jit(solution)/shard_map/all_gather | solution.py:60
  49.9 1.9 %copy.19 = bf16[384,2048]{0,1:T(8,128)(2,1)S(1)} copy(bf16[384,2048]{1,0:T(8,128)(2,1)} %param.8) | data formatting | bytes 3145728 | tf_op args[0]
  51.8 1.0 copy.21
  52.8 2.0 %broadcast_in_dim.53 = f32[2,8,384,128]{3,2,1,0:T(8,128)} broadcast(f32[]{:T(128)} %constant.68.clone.1), dimensions={} | broadcast | bytes 3145732 | tf_op jit(solution)/shard_map/broadcast_in_dim | solution.py:58
  54.8 0.0 copy-done.2
  54.8 38.4 %while.18 = (s32[]{:T(128)}, f32[2,8,384]{2,1,0:T(8,128)S(1)}, f32[2,8,384]{2,1,0:T(8,128)S(1)}, f32[2,8,384,128]{3,2,1,0:T(8,128)}, s32[1536]{0:T(1024)S(1)}, /...) while((s32[]{:T(128)}, f32[2,8,384]{2,1,0:T(8,128)S(1)}, ...), condition=%wide.region_6.7_spmd.clone, body=%wide.region_0.6_spmd.clone.sunk | while | flops 1240953984 | bytes 63517816 | solution.py:82
  54.8 0.1 broadcast_compare_fusion.2
  54.9 0.9 fusion.19
  56.4 10.6 %conditional.3 = ((f32[2,8,384]{2,1,0:T(8,128)S(1)}, f32[2,8,384]{2,1,0:T(8,128)S(1)}, f32[2,8,384,128]{3,2,1,0:T(8,128)})) conditional(s32[]{:T(128)} %convert_element_type.33, (f32[2,8,384]{2,1,0:T(8,128)S(1)}, f32[2,8,384]{2,1,0:T(8,128)S(1)}, f32[2,8,384,128]{3,2,1,0:T(8,128)}) %tuple.60, (pred[384,384]{0,1:T(8,128)(4,1)S(1)}, ...), branch_computations={%region_2.0_spmd, %region_3.5_spmd} | conditional | flops 1240215552 | bytes 63357020 | solution.py:46
  56.4 1.1 %constant_dynamic-slice_fusion = (bf16[384,256]{0,1:T(8,128)(2,1)S(1)}, bf16[384,256]{0,1:T(8,128)(2,1)S(1)}) fusion(bf16[1536,256]{0,1:T(8,128)(2,1)} %get-tuple-element.240, s32[]{:T(128)} %get-tuple-element.236, bf16[1536,256]{0,1:T(8,128)(2,1)} %get-tuple-element.235), kind=kLoop, calls=%fused_computation.11 | loop fusion | bytes 786436 | tf_op jit(solution)/shard_map/while/body/eval_jaxpr/dynamic_slice | solution.py:69
  57.5 1.7 %fusion.2 = (f32[2,8,384]{2,1,0:T(8,128)S(1)}, f32[2,384,384,8]{2,1,3,0:T(8,128)S(1)}) fusion(pred[384,384]{0,1:T(8,128)(4,1)S(1)} %get-tuple-element.234, bf16[384,2,128,1]{0,2,3,1:T(8,128)(2,1)S(1)} %bitcast.34, bf16[384,2,8,128]{3,0,2,1:T(8,128)(2,1)S(1)} %get-tuple-element.237), kind=kOutput, calls=%fused_computation.3 | convolution fusion | flops 611051520 | bytes 11378688 | tf_op jit(solution)/shard_map/while/body/eval_jaxpr/cond/branch_1_fun/qhgd,khd->hgqk/dot_general | solution.py:30
  59.2 0.0 copy-start
  59.2 2.3 %fusion.4 = f32[2,8,384]{2,1,0:T(8,128)S(1)} fusion(f32[2,384,384,8]{2,1,3,0:T(8,128)S(1)} %get-tuple-element.332, f32[2,8,384]{2,1,0:T(8,128)S(1)} %max.4, pred[384,384]{0,1:T(8,128)(4,1)S(1)} %get-tuple-element.234), kind=kLoop, calls=%fused_computation.5 | loop fusion | flops 11790336 | bytes 9633792 | tf_op jit(solution)/shard_map/while/body/eval_jaxpr/cond/branch_1_fun/reduce_sum | solution.py:37
  61.5 0.0 copy-done
  61.5 3.8 %multiply_add_fusion = f32[2,8,384,128]{3,2,1,0:T(8,128)S(1)} fusion(f32[2,8,384,128]{3,2,1,0:T(8,128)S(1)} %copy-done, bf16[384,2,128,1]{0,2,3,1:T(8,128)(2,1)S(1)} %bitcast.37, f32[2,384,384,8]{2,1,3,0:T(8,128)S(1)} %get-tuple-element.332, f32[2,8,384]{2,1,0:T(8,128)S(1)} %max.4, pred[384,384]{0,1:T(8,128)(4,1)S(1)} %get-tuple-element.234, ...), kind=kOutput, calls=%fused_computation.8 | convolution fusion | flops 617349120 | bytes 16121856 | tf_op jit(solution)/shard_map/while/body/eval_jaxpr/cond/branch_1_fun/hgqk,khd->hgqd/dot_general | solution.py:38
  65.4 0.0 copy-start.1
  65.4 1.6 %copy-done.1 = f32[2,8,384,128]{3,2,1,0:T(8,128)} copy-done((f32[2,8,384,128]{3,2,1,0:T(8,128)}, f32[2,8,384,128]{3,2,1,0:T(8,128)S(1)}, u32[]{:S(2)}) %copy-start.1) | copy-done | bytes 3145752 | tf_op jit(solution)/shard_map/while/body/eval_jaxpr/cond
  67.0 0.1 broadcast_compare_fusion.2
  67.1 0.9 fusion.19
  68.6 10.6 %conditional.3 = ((f32[2,8,384]{2,1,0:T(8,128)S(1)}, f32[2,8,384]{2,1,0:T(8,128)S(1)}, f32[2,8,384,128]{3,2,1,0:T(8,128)})) conditional(s32[]{:T(128)} %convert_element_type.33, (f32[2,8,384]{2,1,0:T(8,128)S(1)}, f32[2,8,384]{2,1,0:T(8,128)S(1)}, f32[2,8,384,128]{3,2,1,0:T(8,128)}) %tuple.60, (pred[384,384]{0,1:T(8,128)(4,1)S(1)}, ...), branch_computations={%region_2.0_spmd, %region_3.5_spmd} | conditional | flops 1240215552 | bytes 63357020 | solution.py:46
  68.6 1.1 %constant_dynamic-slice_fusion = (bf16[384,256]{0,1:T(8,128)(2,1)S(1)}, bf16[384,256]{0,1:T(8,128)(2,1)S(1)}) fusion(bf16[1536,256]{0,1:T(8,128)(2,1)} %get-tuple-element.240, s32[]{:T(128)} %get-tuple-element.236, bf16[1536,256]{0,1:T(8,128)(2,1)} %get-tuple-element.235), kind=kLoop, calls=%fused_computation.11 | loop fusion | bytes 786436 | tf_op jit(solution)/shard_map/while/body/eval_jaxpr/dynamic_slice | solution.py:69
  69.7 1.7 %fusion.2 = (f32[2,8,384]{2,1,0:T(8,128)S(1)}, f32[2,384,384,8]{2,1,3,0:T(8,128)S(1)}) fusion(pred[384,384]{0,1:T(8,128)(4,1)S(1)} %get-tuple-element.234, bf16[384,2,128,1]{0,2,3,1:T(8,128)(2,1)S(1)} %bitcast.34, bf16[384,2,8,128]{3,0,2,1:T(8,128)(2,1)S(1)} %get-tuple-element.237), kind=kOutput, calls=%fused_computation.3 | convolution fusion | flops 611051520 | bytes 11378688 | tf_op jit(solution)/shard_map/while/body/eval_jaxpr/cond/branch_1_fun/qhgd,khd->hgqk/dot_general | solution.py:30
  71.4 0.0 copy-start
  71.5 2.3 %fusion.4 = f32[2,8,384]{2,1,0:T(8,128)S(1)} fusion(f32[2,384,384,8]{2,1,3,0:T(8,128)S(1)} %get-tuple-element.332, f32[2,8,384]{2,1,0:T(8,128)S(1)} %max.4, pred[384,384]{0,1:T(8,128)(4,1)S(1)} %get-tuple-element.234), kind=kLoop, calls=%fused_computation.5 | loop fusion | flops 11790336 | bytes 9633792 | tf_op jit(solution)/shard_map/while/body/eval_jaxpr/cond/branch_1_fun/reduce_sum | solution.py:37
  73.8 0.0 copy-done
  73.8 3.8 %multiply_add_fusion = f32[2,8,384,128]{3,2,1,0:T(8,128)S(1)} fusion(f32[2,8,384,128]{3,2,1,0:T(8,128)S(1)} %copy-done, bf16[384,2,128,1]{0,2,3,1:T(8,128)(2,1)S(1)} %bitcast.37, f32[2,384,384,8]{2,1,3,0:T(8,128)S(1)} %get-tuple-element.332, f32[2,8,384]{2,1,0:T(8,128)S(1)} %max.4, pred[384,384]{0,1:T(8,128)(4,1)S(1)} %get-tuple-element.234, ...), kind=kOutput, calls=%fused_computation.8 | convolution fusion | flops 617349120 | bytes 16121856 | tf_op jit(solution)/shard_map/while/body/eval_jaxpr/cond/branch_1_fun/hgqk,khd->hgqd/dot_general | solution.py:38
  77.6 0.0 copy-start.1
  77.6 1.6 %copy-done.1 = f32[2,8,384,128]{3,2,1,0:T(8,128)} copy-done((f32[2,8,384,128]{3,2,1,0:T(8,128)}, f32[2,8,384,128]{3,2,1,0:T(8,128)S(1)}, u32[]{:S(2)}) %copy-start.1) | copy-done | bytes 3145752 | tf_op jit(solution)/shard_map/while/body/eval_jaxpr/cond
  79.3 0.1 broadcast_compare_fusion.2
  79.4 0.9 fusion.19
  80.9 10.6 %conditional.3 = ((f32[2,8,384]{2,1,0:T(8,128)S(1)}, f32[2,8,384]{2,1,0:T(8,128)S(1)}, f32[2,8,384,128]{3,2,1,0:T(8,128)})) conditional(s32[]{:T(128)} %convert_element_type.33, (f32[2,8,384]{2,1,0:T(8,128)S(1)}, f32[2,8,384]{2,1,0:T(8,128)S(1)}, f32[2,8,384,128]{3,2,1,0:T(8,128)}) %tuple.60, (pred[384,384]{0,1:T(8,128)(4,1)S(1)}, ...), branch_computations={%region_2.0_spmd, %region_3.5_spmd} | conditional | flops 1240215552 | bytes 63357020 | solution.py:46
  80.9 1.1 %constant_dynamic-slice_fusion = (bf16[384,256]{0,1:T(8,128)(2,1)S(1)}, bf16[384,256]{0,1:T(8,128)(2,1)S(1)}) fusion(bf16[1536,256]{0,1:T(8,128)(2,1)} %get-tuple-element.240, s32[]{:T(128)} %get-tuple-element.236, bf16[1536,256]{0,1:T(8,128)(2,1)} %get-tuple-element.235), kind=kLoop, calls=%fused_computation.11 | loop fusion | bytes 786436 | tf_op jit(solution)/shard_map/while/body/eval_jaxpr/dynamic_slice | solution.py:69
  82.0 1.7 %fusion.2 = (f32[2,8,384]{2,1,0:T(8,128)S(1)}, f32[2,384,384,8]{2,1,3,0:T(8,128)S(1)}) fusion(pred[384,384]{0,1:T(8,128)(4,1)S(1)} %get-tuple-element.234, bf16[384,2,128,1]{0,2,3,1:T(8,128)(2,1)S(1)} %bitcast.34, bf16[384,2,8,128]{3,0,2,1:T(8,128)(2,1)S(1)} %get-tuple-element.237), kind=kOutput, calls=%fused_computation.3 | convolution fusion | flops 611051520 | bytes 11378688 | tf_op jit(solution)/shard_map/while/body/eval_jaxpr/cond/branch_1_fun/qhgd,khd->hgqk/dot_general | solution.py:30
  83.7 0.0 copy-start
  83.7 2.3 %fusion.4 = f32[2,8,384]{2,1,0:T(8,128)S(1)} fusion(f32[2,384,384,8]{2,1,3,0:T(8,128)S(1)} %get-tuple-element.332, f32[2,8,384]{2,1,0:T(8,128)S(1)} %max.4, pred[384,384]{0,1:T(8,128)(4,1)S(1)} %get-tuple-element.234), kind=kLoop, calls=%fused_computation.5 | loop fusion | flops 11790336 | bytes 9633792 | tf_op jit(solution)/shard_map/while/body/eval_jaxpr/cond/branch_1_fun/reduce_sum | solution.py:37
  86.0 0.0 copy-done
  86.0 3.8 %multiply_add_fusion = f32[2,8,384,128]{3,2,1,0:T(8,128)S(1)} fusion(f32[2,8,384,128]{3,2,1,0:T(8,128)S(1)} %copy-done, bf16[384,2,128,1]{0,2,3,1:T(8,128)(2,1)S(1)} %bitcast.37, f32[2,384,384,8]{2,1,3,0:T(8,128)S(1)} %get-tuple-element.332, f32[2,8,384]{2,1,0:T(8,128)S(1)} %max.4, pred[384,384]{0,1:T(8,128)(4,1)S(1)} %get-tuple-element.234, ...), kind=kOutput, calls=%fused_computation.8 | convolution fusion | flops 617349120 | bytes 16121856 | tf_op jit(solution)/shard_map/while/body/eval_jaxpr/cond/branch_1_fun/hgqk,khd->hgqd/dot_general | solution.py:38
  89.9 1.6 %copy-done.1 = f32[2,8,384,128]{3,2,1,0:T(8,128)} copy-done((f32[2,8,384,128]{3,2,1,0:T(8,128)}, f32[2,8,384,128]{3,2,1,0:T(8,128)S(1)}, u32[]{:S(2)}) %copy-start.1) | copy-done | bytes 3145752 | tf_op jit(solution)/shard_map/while/body/eval_jaxpr/cond
  91.5 0.1 broadcast_compare_fusion.2
  91.6 0.9 fusion.19
  93.2 2.4 %fusion.13 = bf16[384,2,8,128]{3,0,2,1:T(8,128)(2,1)S(1)} fusion(f32[2,8,384,128]{3,2,1,0:T(8,128)} %get-tuple-element.257, f32[2,8,384]{2,1,0:T(8,128)S(1)} %get-tuple-element.258), kind=kLoop, calls=%fused_computation.22 | loop fusion | flops 1572864 | bytes 4743168 | tf_op jit(solution)/shard_map/convert_element_type | solution.py:86
  95.6 1.0 %copy.22 = bf16[384,2,8,128]{3,2,1,0:T(8,128)(2,1)S(1)} copy(bf16[384,2,8,128]{3,0,2,1:T(8,128)(2,1)S(1)} %fusion.13) | data formatting | bytes 3145728 | tf_op jit(solution)/shard_map/convert_element_type | solution.py:86
  96.6 1.6 %copy.32 = bf16[48,8,16,128]{3,1,2,0:T(8,128)(2,1)} copy(bf16[48,8,16,128]{3,2,1,0:T(8,128)(2,1)S(1)} %bitcast.35) | data formatting | bytes 3145728
  (20 shorter events, 0.1 us)
Async XLA Ops:
  49.9 4.9 %copy-start.2 = (s32[384]{0:T(512)S(1)}, s32[384]{0:T(512)}, u32[]{:S(2)}) copy-start(s32[384]{0:T(512)} %param.11) | copy-start | bytes 4612
  59.2 2.3 %copy-start = (f32[2,8,384,128]{3,2,1,0:T(8,128)S(1)}, f32[2,8,384,128]{3,2,1,0:T(8,128)}, u32[]{:S(2)}) copy-start(f32[2,8,384,128]{3,2,1,0:T(8,128)} %get-tuple-element.239) | copy-start | bytes 9437188 | tf_op jit(solution)/shard_map/while/body/eval_jaxpr/cond
  65.4 1.7 %copy-start.1 = (f32[2,8,384,128]{3,2,1,0:T(8,128)}, f32[2,8,384,128]{3,2,1,0:T(8,128)S(1)}, u32[]{:S(2)}) copy-start(f32[2,8,384,128]{3,2,1,0:T(8,128)S(1)} %multiply_add_fusion) | copy-start | bytes 9437188 | tf_op jit(solution)/shard_map/while/body/eval_jaxpr/cond
  71.4 2.3 %copy-start = (f32[2,8,384,128]{3,2,1,0:T(8,128)S(1)}, f32[2,8,384,128]{3,2,1,0:T(8,128)}, u32[]{:S(2)}) copy-start(f32[2,8,384,128]{3,2,1,0:T(8,128)} %get-tuple-element.239) | copy-start | bytes 9437188 | tf_op jit(solution)/shard_map/while/body/eval_jaxpr/cond
  77.6 1.7 %copy-start.1 = (f32[2,8,384,128]{3,2,1,0:T(8,128)}, f32[2,8,384,128]{3,2,1,0:T(8,128)S(1)}, u32[]{:S(2)}) copy-start(f32[2,8,384,128]{3,2,1,0:T(8,128)S(1)} %multiply_add_fusion) | copy-start | bytes 9437188 | tf_op jit(solution)/shard_map/while/body/eval_jaxpr/cond
  83.7 2.3 %copy-start = (f32[2,8,384,128]{3,2,1,0:T(8,128)S(1)}, f32[2,8,384,128]{3,2,1,0:T(8,128)}, u32[]{:S(2)}) copy-start(f32[2,8,384,128]{3,2,1,0:T(8,128)} %get-tuple-element.239) | copy-start | bytes 9437188 | tf_op jit(solution)/shard_map/while/body/eval_jaxpr/cond
  89.9 1.7 %copy-start.1 = (f32[2,8,384,128]{3,2,1,0:T(8,128)}, f32[2,8,384,128]{3,2,1,0:T(8,128)S(1)}, u32[]{:S(2)}) copy-start(f32[2,8,384,128]{3,2,1,0:T(8,128)S(1)} %multiply_add_fusion) | copy-start | bytes 9437188 | tf_op jit(solution)/shard_map/while/body/eval_jaxpr/cond
where the time goes:
time: 98.4 us; the launch traced here: 98.1 us
  blocking collectives  47 us (48%)
  local copies, waits for them, and re-layouts  18.5 us (19%)
  matrix products  16.6 us (17%)
  other arithmetic  13.2 us (13%)
  loops' own time  2.79 us (3%)
    all_gather x1, blocking collectives, per_device(): value_all = lax.all_gather(values, 'ctx', axis=0, tiled=True)  18.8 us
    all_gather x1, blocking collectives, per_device(): key_all = lax.all_gather(keys, 'ctx', axis=0, tiled=True)  17.9 us
    dot_general x3, matrix products, compute(): jnp.einsum('hgqk,khd->hgqd', weights.astype(jnp.bfloat16), value_heads, p...  11.5 us
    all_gather x1, blocking collectives, per_device(): segment_all = lax.all_gather(segment_ids, 'ctx', axis=0, tiled=True)  10.3 us
    unnamed x9, local copies, waits for them, and re-layouts  7.27 us
    reduce_sum x3, other arithmetic, compute(): new_total = row_total * factor + jnp.sum(weights, axis=-1)  6.83 us
    dot_general x3, matrix products, compute(): jnp.einsum('qhgd,khd->hgqk', query_heads, key_heads, preferred_element_ty...  5.11 us
    cond x15, local copies, waits for them, and re-layouts  4.98 us

commit v1 on v0

--- a/solution.py
+++ b/solution.py
@@ -5,6 +5,12 @@
 
 HEAD_DIM = 128
 GROUP = 8
+
+
+def in_order(blocks, dim):
+    dims = list(blocks.shape[1:])
+    dims[dim] *= blocks.shape[0]
+    return jnp.moveaxis(blocks, 0, dim).reshape(dims)
 
 
 def attend_block(
@@ -57,7 +63,19 @@
         jnp.zeros((heads_here, GROUP, row_count), jnp.float32),
         jnp.zeros((heads_here, GROUP, row_count, HEAD_DIM), jnp.float32),
     )
-    key_all = lax.all_gather(keys, "ctx", axis=0, tiled=True)
+    peers = lax.axis_size("ctx")
+    pairs = [(i, (i + 1) % peers) for i in range(peers)]
+    back = [(b, a) for a, b in pairs]
+    lower, upper = ([], [])
+    for step in range(peers - 1):
+        if step % 2 == 0:
+            lower.append(lax.ppermute(lower[-1] if lower else keys, "ctx", pairs))
+        else:
+            upper.append(lax.ppermute(upper[-1] if upper else keys, "ctx", back))
+    pieces = jnp.stack([*lower[::-1], keys, *upper])
+    shift = lax.axis_index("ctx") - len(lower)
+    pieces = pieces[(jnp.arange(peers) - shift) % peers]
+    key_all = in_order(pieces, 0)
     value_all = lax.all_gather(values, "ctx", axis=0, tiled=True)
     segment_all = lax.all_gather(segment_ids, "ctx", axis=0, tiled=True)
     blocks = max(1, key_all.shape[0] // row_count)

time: 98.4 us -> 92.4 us (0.939)
  blocking collectives: 47 us -> 32.2 us
  starting transfers between devices: 0 us -> 4.42 us
  waiting for transfers between devices: 0 us -> 3.47 us
  local copies, waits for them, and re-layouts: 18.5 us -> 17.2 us
  other arithmetic: 13.2 us -> 14.4 us
    all_gather x1 -> x0, blocking collectives: 17.9 us -> none  [per_device(): key_all = lax.all_gather(keys, 'ctx', axis=0, tiled=True)]
    ppermute x0 -> x3, starting transfers between devices: none -> 4.42 us  [the longest x2 3.97 us: per_device(): lower.append(lax.ppermute(lower[-1] if lower else keys, 'ctx', pairs))]
    all_gather x1, blocking collectives: 10.3 us -> 14.4 us  [per_device(): segment_all = lax.all_gather(segment_ids, 'ctx', axis=0, tiled=True)]
    ppermute x0 -> x3, waiting for transfers between devices: none -> 3.47 us  [the longest x2 3.47 us: per_device(): lower.append(lax.ppermute(lower[-1] if lower else keys, 'ctx', pairs))]
    dynamic_slice x3, local copies, waits for them, and re-layouts: 3.21 us -> 0.15 us  [turn(): value_part = lax.dynamic_slice_in_dim(value_all, offset, width_rows, 0)]
    gather x0 -> x1, local copies, waits for them, and re-layouts: none -> 1.48 us  [per_device(): pieces = pieces[(jnp.arange(peers) - shift) % peers]]
    reshape x0 -> x1, local copies, waits for them, and re-layouts: none -> 1.41 us  [in_order(): return jnp.moveaxis(blocks, 0, dim).reshape(dims)]
    another operation x0 -> x1, other arithmetic: none -> 1.12 us  [per_device(): pieces = jnp.stack([*lower[::-1], keys, *upper])]
  transfers between devices with their start and end apart: 0 -> 3, of which waited for: 0 -> 1; matrix products, arithmetic and copies ran while one was open for 0% -> 5% of each run, Pallas kernels for 0% -> 0%
where the time goes in v1:
time: 92.4 us; the launch traced here: 91.2 us
  blocking collectives  32.2 us (35%)
  local copies, waits for them, and re-layouts  17.2 us (19%)
  matrix products  16.6 us (18%)
  other arithmetic  14.4 us (16%)
  starting transfers between devices  4.42 us (5%)
  waiting for transfers between devices  3.47 us (4%)
  loops' own time  2.85 us (3%)
    all_gather x1, blocking collectives, per_device(): value_all = lax.all_gather(values, 'ctx', axis=0, tiled=True)  17.8 us
    all_gather x1, blocking collectives, per_device(): segment_all = lax.all_gather(segment_ids, 'ctx', axis=0, tiled=True)  14.4 us
    dot_general x3, matrix products, compute(): jnp.einsum('hgqk,khd->hgqd', weights.astype(jnp.bfloat16), value_heads, p...  11.5 us
    reduce_sum x3, other arithmetic, compute(): new_total = row_total * factor + jnp.sum(weights, axis=-1)  6.83 us
    unnamed x10, local copies, waits for them, and re-layouts  6.18 us
    dot_general x3, matrix products, compute(): jnp.einsum('qhgd,khd->hgqk', query_heads, key_heads, preferred_element_ty...  5.11 us
    cond x15, local copies, waits for them, and re-layouts  4.97 us
    ppermute x2, starting transfers between devices, per_device(): lower.append(lax.ppermute(lower[-1] if lower else keys, 'ctx', pairs))  3.97 us
  transfers between devices with their start and end apart: 3, of which 1 were waited for; matrix products, arithmetic and copies ran while one was open for 5% of the time, Pallas kernels for 0%

profile of v1, /device:TPU:22, one launch (start us, length us, event | category | flops | bytes accessed | tf_op | source)
XLA Modules:
  0.0 91.2 jit_solution(15544225637767907696)
XLA Ops:
  0.0 1.6 %collective-permute-start = (bf16[384,256]{1,0:T(8,128)(2,1)}, bf16[384,256]{1,0:T(8,128)(2,1)}, u32[]{:S(2)}, u32[]{:S(2)}) collective-permute-start(bf16[384,256]{1,0:T(8,128)(2,1)} %param.9), channel_id=1, source_target_pairs={{0,4},{4,8},{8,12},{12,0},{1,5},{5,9},{9,13},{13,1},{2,6},{6,10},{... | collective-permute-start | bytes 589832 | tf_op jit(solution)/shard_map/ppermute | solution.py:72
  1.6 0.4 collective-permute-start.2
  2.0 0.7 reshape.100
  2.7 14.4 %all-gather = s32[4,1,384]{2,1,0:T(1,128)S(1)} all-gather(s32[1,1,384]{2,1,0:T(1,128)S(1)} %reshape.100), channel_id=1, replica_groups=mesh['groups'=2,'ctx'=4,'tp'=2,'sub'=2] {'ctx'}, dimensions={0}, use_global_device_ids=true | all-gather | bytes 7680 | tf_op jit(solution)/shard_map/all_gather | solution.py:80
  17.2 1.1 %copy.20 = bf16[384,256]{0,1:T(8,128)(2,1)S(1)} copy(bf16[384,256]{1,0:T(8,128)(2,1)} %param.10) | data formatting | bytes 393216 | tf_op args[2]
  18.3 1.9 %copy.19 = bf16[384,2048]{0,1:T(8,128)(2,1)S(1)} copy(bf16[384,2048]{1,0:T(8,128)(2,1)} %param.8) | data formatting | bytes 3145728 | tf_op args[0]
  20.2 1.0 %copy.21 = bf16[384,2,8,128]{3,0,2,1:T(8,128)(2,1)S(1)} copy(bf16[384,2,8,128]{0,3,2,1:T(8,128)(2,1)S(1)} %bitcast.43) | data formatting | bytes 3145728
  21.1 0.0 copy-start.3
  21.2 17.8 %all_gather.7 = bf16[1536,256]{0,1:T(8,128)(2,1)S(1)} all-gather(bf16[384,256]{0,1:T(8,128)(2,1)S(1)} %copy.20), channel_id=1, replica_groups=mesh['groups'=2,'ctx'=4,'tp'=2,'sub'=2] {'ctx'}, dimensions={0}, use_global_device_ids=true | all-gather | bytes 983040 | tf_op jit(solution)/shard_map/all_gather | solution.py:79
  38.9 2.4 %collective-permute-start.1 = (bf16[384,256]{1,0:T(8,128)(2,1)}, bf16[384,256]{1,0:T(8,128)(2,1)S(1)}, u32[]{:S(2)}, u32[]{:S(2)}) collective-permute-start(bf16[384,256]{1,0:T(8,128)(2,1)} %collective-permute-done), channel_id=1, source_target_pairs={{0,4},{4,8},{8,12},{12,0},{1,5},{5,9},{9,13},{13,1},{2,6},{6,10},{... | collective-permute-start | bytes 589832 | tf_op jit(solution)/shard_map/ppermute | solution.py:72
  41.4 3.5 %collective-permute-done.1 = bf16[384,256]{1,0:T(8,128)(2,1)S(1)} collective-permute-done((bf16[384,256]{1,0:T(8,128)(2,1)}, bf16[384,256]{1,0:T(8,128)(2,1)S(1)}, u32[]{:S(2)}, u32[]{:S(2)}) %collective-permute-start.1) | collective-permute-done | bytes 196640 | tf_op jit(solution)/shard_map/ppermute | solution.py:72
  44.8 1.1 %pad_maximum_fusion = bf16[4,384,256]{2,1,0:T(8,128)(2,1)S(1)} fusion(bf16[1,384,256]{2,1,0:T(8,128)(2,1)} %bitcast.8, bf16[1,384,256]{2,1,0:T(8,128)(2,1)S(1)} %bitcast.46, bf16[1,384,256]{2,1,0:T(8,128)(2,1)} %bitcast.6, bf16[1,384,256]{2,1,0:T(8,128)(2,1)S(1)} %bitcast.47), kind=kLoop, calls=%fused_computation.24 | loop fusion | flops 1179648 | bytes 1572864 | tf_op jit(solution)/shard_map/stack | solution.py:75
  45.9 1.5 %gather_fusion = bf16[4,384,256]{2,1,0:T(8,128)(2,1)} fusion(bf16[4,384,256]{2,1,0:T(8,128)(2,1)S(1)} %pad_maximum_fusion, s32[1024]{0:T(1024)S(1)} %pad_clamp_fusion), kind=kCustom, calls=%fused_computation | custom fusion | bytes 1572880 | tf_op jit(solution)/shard_map/gather | solution.py:77
  47.4 1.4 %copy.30 = bf16[1536,256]{0,1:T(8,128)(2,1)S(1)} copy(bf16[1536,256]{1,0:T(8,128)(2,1)} %bitcast.45) | data formatting | bytes 1572864 | tf_op jit(solution)/shard_map/reshape | solution.py:13
  48.9 2.0 %broadcast_in_dim.54 = f32[2,8,384,128]{3,2,1,0:T(8,128)} broadcast(f32[]{:T(128)} %constant.84.clone.1), dimensions={} | broadcast | bytes 3145732 | tf_op jit(solution)/shard_map/broadcast_in_dim | solution.py:64
  50.8 35.4 %while.18 = (s32[]{:T(128)}, f32[2,8,384]{2,1,0:T(8,128)S(1)}, f32[2,8,384]{2,1,0:T(8,128)S(1)}, f32[2,8,384,128]{3,2,1,0:T(8,128)}, s32[1536]{0:T(1024)S(1)}, /...) while((s32[]{:T(128)}, f32[2,8,384]{2,1,0:T(8,128)S(1)}, ...), condition=%wide.region_6.7_spmd.clone, body=%wide.region_0.6_spmd.clone.sunk | while | flops 1240953984 | bytes 63517816 | solution.py:100
  50.8 0.1 broadcast_compare_fusion.2
  50.9 0.9 fusion.21
  52.5 9.6 %conditional.3 = ((f32[2,8,384]{2,1,0:T(8,128)S(1)}, f32[2,8,384]{2,1,0:T(8,128)S(1)}, f32[2,8,384,128]{3,2,1,0:T(8,128)})) conditional(s32[]{:T(128)} %convert_element_type.33, (f32[2,8,384]{2,1,0:T(8,128)S(1)}, f32[2,8,384]{2,1,0:T(8,128)S(1)}, f32[2,8,384,128]{3,2,1,0:T(8,128)}) %tuple.60, (pred[384,384]{0,1:T(8,128)(4,1)S(1)}, ...), branch_computations={%region_2.2_spmd, %region_3.5_spmd} | conditional | flops 1240215552 | bytes 63357020 | solution.py:52
  52.5 0.1 constant_dynamic-slice_fusion
  52.5 1.7 %fusion.2 = (f32[2,8,384]{2,1,0:T(8,128)S(1)}, f32[2,384,384,8]{2,1,3,0:T(8,128)S(1)}) fusion(pred[384,384]{0,1:T(8,128)(4,1)S(1)} %get-tuple-element.234, bf16[384,2,128,1]{0,2,3,1:T(8,128)(2,1)S(1)} %bitcast.41, bf16[384,2,8,128]{3,0,2,1:T(8,128)(2,1)S(1)} %get-tuple-element.237), kind=kOutput, calls=%fused_computation.4 | convolution fusion | flops 611051520 | bytes 11378688 | tf_op jit(solution)/shard_map/while/body/eval_jaxpr/cond/branch_1_fun/qhgd,khd->hgqk/dot_general | solution.py:36
  54.3 0.0 copy-start
  54.3 2.3 %fusion.4 = f32[2,8,384]{2,1,0:T(8,128)S(1)} fusion(f32[2,384,384,8]{2,1,3,0:T(8,128)S(1)} %get-tuple-element.332, f32[2,8,384]{2,1,0:T(8,128)S(1)} %max.4, pred[384,384]{0,1:T(8,128)(4,1)S(1)} %get-tuple-element.234), kind=kLoop, calls=%fused_computation.6 | loop fusion | flops 11790336 | bytes 9633792 | tf_op jit(solution)/shard_map/while/body/eval_jaxpr/cond/branch_1_fun/reduce_sum | solution.py:43
  56.6 3.8 %multiply_add_fusion = f32[2,8,384,128]{3,2,1,0:T(8,128)S(1)} fusion(f32[2,8,384,128]{3,2,1,0:T(8,128)S(1)} %copy-done, bf16[384,2,128,1]{0,2,3,1:T(8,128)(2,1)S(1)} %bitcast.44, f32[2,384,384,8]{2,1,3,0:T(8,128)S(1)} %get-tuple-element.332, f32[2,8,384]{2,1,0:T(8,128)S(1)} %max.4, pred[384,384]{0,1:T(8,128)(4,1)S(1)} %get-tuple-element.234, ...), kind=kOutput, calls=%fused_computation.9 | convolution fusion | flops 617349120 | bytes 16121856 | tf_op jit(solution)/shard_map/while/body/eval_jaxpr/cond/branch_1_fun/hgqk,khd->hgqd/dot_general | solution.py:44
  60.5 1.6 %copy-done.1 = f32[2,8,384,128]{3,2,1,0:T(8,128)} copy-done((f32[2,8,384,128]{3,2,1,0:T(8,128)}, f32[2,8,384,128]{3,2,1,0:T(8,128)S(1)}, u32[]{:S(2)}) %copy-start.1) | copy-done | bytes 3145752 | tf_op jit(solution)/shard_map/while/body/eval_jaxpr/cond
  62.1 0.1 broadcast_compare_fusion.2
  62.2 0.9 fusion.21
  63.7 9.6 %conditional.3 = ((f32[2,8,384]{2,1,0:T(8,128)S(1)}, f32[2,8,384]{2,1,0:T(8,128)S(1)}, f32[2,8,384,128]{3,2,1,0:T(8,128)})) conditional(s32[]{:T(128)} %convert_element_type.33, (f32[2,8,384]{2,1,0:T(8,128)S(1)}, f32[2,8,384]{2,1,0:T(8,128)S(1)}, f32[2,8,384,128]{3,2,1,0:T(8,128)}) %tuple.60, (pred[384,384]{0,1:T(8,128)(4,1)S(1)}, ...), branch_computations={%region_2.2_spmd, %region_3.5_spmd} | conditional | flops 1240215552 | bytes 63357020 | solution.py:52
  63.7 0.1 constant_dynamic-slice_fusion
  63.8 1.7 %fusion.2 = (f32[2,8,384]{2,1,0:T(8,128)S(1)}, f32[2,384,384,8]{2,1,3,0:T(8,128)S(1)}) fusion(pred[384,384]{0,1:T(8,128)(4,1)S(1)} %get-tuple-element.234, bf16[384,2,128,1]{0,2,3,1:T(8,128)(2,1)S(1)} %bitcast.41, bf16[384,2,8,128]{3,0,2,1:T(8,128)(2,1)S(1)} %get-tuple-element.237), kind=kOutput, calls=%fused_computation.4 | convolution fusion | flops 611051520 | bytes 11378688 | tf_op jit(solution)/shard_map/while/body/eval_jaxpr/cond/branch_1_fun/qhgd,khd->hgqk/dot_general | solution.py:36
  65.5 0.0 copy-start
  65.5 2.3 %fusion.4 = f32[2,8,384]{2,1,0:T(8,128)S(1)} fusion(f32[2,384,384,8]{2,1,3,0:T(8,128)S(1)} %get-tuple-element.332, f32[2,8,384]{2,1,0:T(8,128)S(1)} %max.4, pred[384,384]{0,1:T(8,128)(4,1)S(1)} %get-tuple-element.234), kind=kLoop, calls=%fused_computation.6 | loop fusion | flops 11790336 | bytes 9633792 | tf_op jit(solution)/shard_map/while/body/eval_jaxpr/cond/branch_1_fun/reduce_sum | solution.py:43
  67.9 3.8 %multiply_add_fusion = f32[2,8,384,128]{3,2,1,0:T(8,128)S(1)} fusion(f32[2,8,384,128]{3,2,1,0:T(8,128)S(1)} %copy-done, bf16[384,2,128,1]{0,2,3,1:T(8,128)(2,1)S(1)} %bitcast.44, f32[2,384,384,8]{2,1,3,0:T(8,128)S(1)} %get-tuple-element.332, f32[2,8,384]{2,1,0:T(8,128)S(1)} %max.4, pred[384,384]{0,1:T(8,128)(4,1)S(1)} %get-tuple-element.234, ...), kind=kOutput, calls=%fused_computation.9 | convolution fusion | flops 617349120 | bytes 16121856 | tf_op jit(solution)/shard_map/while/body/eval_jaxpr/cond/branch_1_fun/hgqk,khd->hgqd/dot_general | solution.py:44
  71.7 1.6 %copy-done.1 = f32[2,8,384,128]{3,2,1,0:T(8,128)} copy-done((f32[2,8,384,128]{3,2,1,0:T(8,128)}, f32[2,8,384,128]{3,2,1,0:T(8,128)S(1)}, u32[]{:S(2)}) %copy-start.1) | copy-done | bytes 3145752 | tf_op jit(solution)/shard_map/while/body/eval_jaxpr/cond
  73.4 0.1 broadcast_compare_fusion.2
  73.4 0.9 fusion.21
  75.0 9.6 %conditional.3 = ((f32[2,8,384]{2,1,0:T(8,128)S(1)}, f32[2,8,384]{2,1,0:T(8,128)S(1)}, f32[2,8,384,128]{3,2,1,0:T(8,128)})) conditional(s32[]{:T(128)} %convert_element_type.33, (f32[2,8,384]{2,1,0:T(8,128)S(1)}, f32[2,8,384]{2,1,0:T(8,128)S(1)}, f32[2,8,384,128]{3,2,1,0:T(8,128)}) %tuple.60, (pred[384,384]{0,1:T(8,128)(4,1)S(1)}, ...), branch_computations={%region_2.2_spmd, %region_3.5_spmd} | conditional | flops 1240215552 | bytes 63357020 | solution.py:52
  75.0 0.1 constant_dynamic-slice_fusion
  75.1 1.7 %fusion.2 = (f32[2,8,384]{2,1,0:T(8,128)S(1)}, f32[2,384,384,8]{2,1,3,0:T(8,128)S(1)}) fusion(pred[384,384]{0,1:T(8,128)(4,1)S(1)} %get-tuple-element.234, bf16[384,2,128,1]{0,2,3,1:T(8,128)(2,1)S(1)} %bitcast.41, bf16[384,2,8,128]{3,0,2,1:T(8,128)(2,1)S(1)} %get-tuple-element.237), kind=kOutput, calls=%fused_computation.4 | convolution fusion | flops 611051520 | bytes 11378688 | tf_op jit(solution)/shard_map/while/body/eval_jaxpr/cond/branch_1_fun/qhgd,khd->hgqk/dot_general | solution.py:36
  76.8 0.0 copy-start
  76.8 2.3 %fusion.4 = f32[2,8,384]{2,1,0:T(8,128)S(1)} fusion(f32[2,384,384,8]{2,1,3,0:T(8,128)S(1)} %get-tuple-element.332, f32[2,8,384]{2,1,0:T(8,128)S(1)} %max.4, pred[384,384]{0,1:T(8,128)(4,1)S(1)} %get-tuple-element.234), kind=kLoop, calls=%fused_computation.6 | loop fusion | flops 11790336 | bytes 9633792 | tf_op jit(solution)/shard_map/while/body/eval_jaxpr/cond/branch_1_fun/reduce_sum | solution.py:43
  79.1 3.8 %multiply_add_fusion = f32[2,8,384,128]{3,2,1,0:T(8,128)S(1)} fusion(f32[2,8,384,128]{3,2,1,0:T(8,128)S(1)} %copy-done, bf16[384,2,128,1]{0,2,3,1:T(8,128)(2,1)S(1)} %bitcast.44, f32[2,384,384,8]{2,1,3,0:T(8,128)S(1)} %get-tuple-element.332, f32[2,8,384]{2,1,0:T(8,128)S(1)} %max.4, pred[384,384]{0,1:T(8,128)(4,1)S(1)} %get-tuple-element.234, ...), kind=kOutput, calls=%fused_computation.9 | convolution fusion | flops 617349120 | bytes 16121856 | tf_op jit(solution)/shard_map/while/body/eval_jaxpr/cond/branch_1_fun/hgqk,khd->hgqd/dot_general | solution.py:44
  83.0 1.6 %copy-done.1 = f32[2,8,384,128]{3,2,1,0:T(8,128)} copy-done((f32[2,8,384,128]{3,2,1,0:T(8,128)}, f32[2,8,384,128]{3,2,1,0:T(8,128)S(1)}, u32[]{:S(2)}) %copy-start.1) | copy-done | bytes 3145752 | tf_op jit(solution)/shard_map/while/body/eval_jaxpr/cond
  84.6 0.1 broadcast_compare_fusion.2
  84.7 0.9 fusion.21
  86.3 2.4 %fusion.13 = bf16[384,2,8,128]{3,0,2,1:T(8,128)(2,1)S(1)} fusion(f32[2,8,384,128]{3,2,1,0:T(8,128)} %get-tuple-element.257, f32[2,8,384]{2,1,0:T(8,128)S(1)} %get-tuple-element.258), kind=kLoop, calls=%fused_computation.23 | loop fusion | flops 1572864 | bytes 4743168 | tf_op jit(solution)/shard_map/convert_element_type | solution.py:104
  88.7 1.0 %copy.22 = bf16[384,2,8,128]{3,2,1,0:T(8,128)(2,1)S(1)} copy(bf16[384,2,8,128]{3,0,2,1:T(8,128)(2,1)S(1)} %fusion.13) | data formatting | bytes 3145728 | tf_op jit(solution)/shard_map/convert_element_type | solution.py:104
  89.7 1.6 %copy.33 = bf16[48,8,16,128]{3,1,2,0:T(8,128)(2,1)} copy(bf16[48,8,16,128]{3,2,1,0:T(8,128)(2,1)S(1)} %bitcast.42) | data formatting | bytes 3145728
  (31 shorter events, 0.2 us)
Async XLA Ops:
  0.0 44.8 %copy-start.2 = (bf16[384,256]{1,0:T(8,128)(2,1)S(1)}, bf16[384,256]{1,0:T(8,128)(2,1)}, u32[]{:S(2)}) copy-start(bf16[384,256]{1,0:T(8,128)(2,1)} %param.9) | copy-start | bytes 589828
  0.0 38.9 %collective-permute-start = (bf16[384,256]{1,0:T(8,128)(2,1)}, bf16[384,256]{1,0:T(8,128)(2,1)}, u32[]{:S(2)}, u32[]{:S(2)}) collective-permute-start(bf16[384,256]{1,0:T(8,128)(2,1)} %param.9), channel_id=1, source_target_pairs={{0,4},{4,8},{8,12},{12,0},{1,5},{5,9},{9,13},{13,1},{2,6},{6,10},{... | collective-permute-start | bytes 589832 | tf_op jit(solution)/shard_map/ppermute | solution.py:72
  1.6 39.8 %collective-permute-start.2 = (bf16[384,256]{1,0:T(8,128)(2,1)}, bf16[384,256]{1,0:T(8,128)(2,1)}, u32[]{:S(2)}, u32[]{:S(2)}) collective-permute-start(bf16[384,256]{1,0:T(8,128)(2,1)} %param.9), channel_id=1, source_target_pairs={{4,0},{8,4},{12,8},{0,12},{5,1},{9,5},{13,9},{1,13},{6,2},{10,6},{... | collective-permute-start | bytes 589832 | tf_op jit(solution)/shard_map/ppermute | solution.py:74
  21.1 29.7 %copy-start.3 = (s32[384]{0:T(512)S(1)}, s32[384]{0:T(512)}, u32[]{:S(2)}) copy-start(s32[384]{0:T(512)} %param.11) | copy-start | bytes 4612
  38.9 5.9 %collective-permute-start.1 = (bf16[384,256]{1,0:T(8,128)(2,1)}, bf16[384,256]{1,0:T(8,128)(2,1)S(1)}, u32[]{:S(2)}, u32[]{:S(2)}) collective-permute-start(bf16[384,256]{1,0:T(8,128)(2,1)} %collective-permute-done), channel_id=1, source_target_pairs={{0,4},{4,8},{8,12},{12,0},{1,5},{5,9},{9,13},{13,1},{2,6},{6,10},{... | collective-permute-start | bytes 589832 | tf_op jit(solution)/shard_map/ppermute | solution.py:72
  54.3 2.3 %copy-start = (f32[2,8,384,128]{3,2,1,0:T(8,128)S(1)}, f32[2,8,384,128]{3,2,1,0:T(8,128)}, u32[]{:S(2)}) copy-start(f32[2,8,384,128]{3,2,1,0:T(8,128)} %get-tuple-element.239) | copy-start | bytes 9437188 | tf_op jit(solution)/shard_map/while/body/eval_jaxpr/cond
  60.4 1.7 %copy-start.1 = (f32[2,8,384,128]{3,2,1,0:T(8,128)}, f32[2,8,384,128]{3,2,1,0:T(8,128)S(1)}, u32[]{:S(2)}) copy-start(f32[2,8,384,128]{3,2,1,0:T(8,128)S(1)} %multiply_add_fusion) | copy-start | bytes 9437188 | tf_op jit(solution)/shard_map/while/body/eval_jaxpr/cond
  65.5 2.3 %copy-start = (f32[2,8,384,128]{3,2,1,0:T(8,128)S(1)}, f32[2,8,384,128]{3,2,1,0:T(8,128)}, u32[]{:S(2)}) copy-start(f32[2,8,384,128]{3,2,1,0:T(8,128)} %get-tuple-element.239) | copy-start | bytes 9437188 | tf_op jit(solution)/shard_map/while/body/eval_jaxpr/cond
  71.7 1.7 %copy-start.1 = (f32[2,8,384,128]{3,2,1,0:T(8,128)}, f32[2,8,384,128]{3,2,1,0:T(8,128)S(1)}, u32[]{:S(2)}) copy-start(f32[2,8,384,128]{3,2,1,0:T(8,128)S(1)} %multiply_add_fusion) | copy-start | bytes 9437188 | tf_op jit(solution)/shard_map/while/body/eval_jaxpr/cond
  76.8 2.3 %copy-start = (f32[2,8,384,128]{3,2,1,0:T(8,128)S(1)}, f32[2,8,384,128]{3,2,1,0:T(8,128)}, u32[]{:S(2)}) copy-start(f32[2,8,384,128]{3,2,1,0:T(8,128)} %get-tuple-element.239) | copy-start | bytes 9437188 | tf_op jit(solution)/shard_map/while/body/eval_jaxpr/cond
  82.9 1.7 %copy-start.1 = (f32[2,8,384,128]{3,2,1,0:T(8,128)}, f32[2,8,384,128]{3,2,1,0:T(8,128)S(1)}, u32[]{:S(2)}) copy-start(f32[2,8,384,128]{3,2,1,0:T(8,128)S(1)} %multiply_add_fusion) | copy-start | bytes 9437188 | tf_op jit(solution)/shard_map/while/body/eval_jaxpr/cond
